TPU v7x, 32 devices: a whole 2x2x4 slice. The times are simulated.
32 devices in a mesh: groups: 2 (over x), gx: 16 (over z, y, core).
Axes of the slice: x: 2, y: 2, z: 4, core: 2. Of those that a mesh axis runs over, the one named last changes fastest.
Arguments:
- volume: bfloat16 [32, 256, 6, 128], P('groups', 'gx'), parts along dimension 0, may hold values from -6 to 6
- conv_weight: bfloat16 [256, 27, 128], P('gx'), may hold values from -0.078125 to 0.078125
- conv_bias: float32 [128], replicated, may hold values from -3 to 3
- tconv_weight: bfloat16 [27, 64, 128], replicated, may hold values from -0.25 to 0.25
Outputs:
- decoded: bfloat16 [64, 64, 12, 256], P(('groups', 'gx')), parts along dimension 0
There are 2 independent parts, one for each index of `groups`. A program takes and returns all parts, laid end to end along the dimension named above; an argument that names none is the same for every part. Nothing has to cross between parts.
All inputs are finite; a program needn't handle non-finite values.
Results may differ from a plain program's by a relative error of at most 0.005.
Values may be sent and summed in bfloat16 or wider, within the bound.
A program may use at most 64 MiB of HBM per device.

v0:
```python
import jax
import jax.numpy as jnp
from jax import lax
from jax.sharding import PartitionSpec as P


def extended(block, sides, width):
    for axis, dim in sides:
        count = lax.axis_size(axis)
        forward = [(i, i + 1) for i in range(count - 1)]
        backward = [(target, source) for source, target in forward]
        low = lax.ppermute(
            lax.slice_in_dim(block, block.shape[dim] - width, None, axis=dim), axis, forward
        )
        high = lax.ppermute(lax.slice_in_dim(block, 0, width, axis=dim), axis, backward)
        block = jnp.concatenate([low, block, high], axis=dim)
    return block


def from_behind(block, axis, distance):
    devices = range(lax.axis_size(axis))
    route = [(i - distance, i) for i in devices if i - distance in devices]
    return lax.ppermute(block, axis, route)


def next_cell(field, axis):
    size = field.shape[axis]
    rest = lax.slice_in_dim(field, 1, size, axis=axis)
    zero_shape = list(field.shape)
    zero_shape[axis] = 1
    return jnp.concatenate([rest, jnp.zeros(zero_shape, field.dtype)], axis=axis)


def yz_classes(products, tap_x):
    layout_options = (((1, False),), ((2, False), (0, True)))
    parity_classes = []
    for par_y in range(2):
        for par_z in range(2):
            total = jnp.zeros(products.shape[:1] + products.shape[4:], jnp.float32)
            for tap_y, shift_y in layout_options[par_y]:
                for tap_z, shift_z in layout_options[par_z]:
                    term = products[:, tap_x, tap_y, tap_z]
                    if shift_y:
                        term = next_cell(term, 2)
                    if shift_z:
                        term = next_cell(term, 3)
                    total = total + term
            parity_classes.append(total)
    return jnp.stack(parity_classes, axis=0)


def alternate(even, odd):
    both = jnp.stack([even, odd], axis=0)
    rows, chans, wide_y, wide_z = (both.shape[2], both.shape[3], both.shape[4], both.shape[5])
    both = both.reshape(2, 2, 2, rows, chans, wide_y, wide_z)
    both = jnp.transpose(both, (3, 0, 4, 5, 1, 6, 2))
    return both.reshape(2 * rows, chans, 2 * wide_y, 2 * wide_z)


def conv_rows(block, weight, count):
    chans, wide_y, wide_z = (block.shape[1], block.shape[2] - 2, block.shape[3] - 2)
    taps = []
    for tap_x in range(3):
        for tap_y in range(3):
            for tap_z in range(3):
                taps.append(
                    block[tap_x : tap_x + count, :, tap_y : tap_y + wide_y, tap_z : tap_z + wide_z]
                )
    patch_columns = jnp.stack(taps, axis=2).reshape(count, chans * 27, wide_y * wide_z)
    flattened_patches = weight.reshape(chans * 27, weight.shape[2])
    output_volume = jnp.einsum(
        "fwh,wb->fbh", patch_columns, flattened_patches, preferred_element_type=jnp.float32
    )
    return output_volume.reshape(count, weight.shape[2], wide_y, wide_z)


def tap_products(hidden, flattened_patches, cup):
    rows, wide_y, wide_z = (hidden.shape[0], hidden.shape[2], hidden.shape[3])
    products = jnp.einsum(
        "oc,ncyz->noyz", flattened_patches, hidden, preferred_element_type=jnp.float32
    )
    return products.reshape(rows, 3, 3, 3, cup, wide_y, wide_z)


def per_device(volume, conv_weight, conv_bias, tconv_weight):
    wide_x, wide_y, wide_z = (volume.shape[0], volume.shape[2], volume.shape[3])
    rows = wide_x // lax.axis_size("gx")
    cout = conv_weight.shape[2]
    local = lax.all_to_all(volume, "gx", split_axis=0, concat_axis=1, tiled=True)
    widened_volume = extended(local, (("gx", 0),), 1)
    padded_volume = jnp.pad(widened_volume, ((0, 0), (0, 0), (1, 1), (1, 1)))
    summed = conv_rows(padded_volume, lax.all_gather(conv_weight, "gx", axis=0, tiled=True), rows)
    hidden = jnp.maximum(summed + conv_bias[None, :, None, None], 0.0).astype(jnp.bfloat16)
    cup = tconv_weight.shape[1]
    flattened_patches = tconv_weight.reshape(27 * cup, cout)
    products = tap_products(hidden, flattened_patches, cup)
    first = yz_classes(products, 0)
    middle = yz_classes(products, 1)
    last = yz_classes(products, 2)
    edge = from_behind(hidden, "gx", -1)
    leading_edge = yz_classes(tap_products(edge, flattened_patches, cup), 0)
    following = jnp.concatenate([first[:, 1:], leading_edge], axis=1)
    odd = last + following
    return alternate(middle, odd).astype(jnp.bfloat16)


def solution(mesh):
    return jax.shard_map(
        per_device,
        mesh=mesh,
        in_specs=(P("groups", "gx", None, None), P("gx", None, None), P(), P()),
        out_specs=P(("groups", "gx"), None, None, None),
        check_vma=False,
    )
```

profile of v0, /device:TPU:5, one launch (start us, length us, event | category | flops | bytes accessed | tf_op | source)
XLA Modules:
  0.0 140.1 jit_solution(13895225849409607237)
XLA Ops:
  6.5 17.9 %all_to_all.12 = bf16[16,16,6,128]{3,1,2,0:T(8,128)(2,1)S(1)} all-to-all(bf16[16,16,6,128]{3,1,2,0:T(8,128)(2,1)} %param.4), channel_id=1, replica_groups=mesh['groups'=2,'gx'=16] {'gx'}, dimensions={0} | all-to-all | bytes 786432 | tf_op jit(solution)/shard_map/all_to_all | solution.py:89
  24.4 3.2 %collective-permute-start = (bf16[1,256,6,128]{3,1,2,0:T(8,128)(2,1)S(1)}, bf16[1,256,6,128]{3,1,2,0:T(8,128)(2,1)S(1)}, u32[]{:S(2)}, u32[]{:S(2)}) collective-permute-start(bf16[1,256,6,128]{3,1,2,0:T(8,128)(2,1)S(1)} %bitcast.296), channel_id=1, source_target_pairs={{0,1},{1,2},{2,3},{3,4},{4,5},{5,6},{6,7},{7,8},{8,9},{9,10},{10,1... | collective-permute-start | bytes 1179656 | tf_op jit(solution)/shard_map/ppermute | solution.py:12
  27.7 1.9 %collective-permute-start.1 = (bf16[1,256,6,128]{3,1,2,0:T(8,128)(2,1)S(1)}, bf16[1,256,6,128]{3,1,2,0:T(8,128)(2,1)S(1)}, u32[]{:S(2)}, u32[]{:S(2)}) collective-permute-start(bf16[1,256,6,128]{3,1,2,0:T(8,128)(2,1)S(1)} %bitcast.297), channel_id=1, source_target_pairs={{1,0},{2,1},{3,2},{4,3},{5,4},{6,5},{7,6},{8,7},{9,8},{10,9},{11,1... | collective-permute-start | bytes 1179656 | tf_op jit(solution)/shard_map/ppermute | solution.py:15
  29.6 2.8 %collective-permute-done = bf16[1,256,6,128]{3,1,2,0:T(8,128)(2,1)S(1)} collective-permute-done((bf16[1,256,6,128]{3,1,2,0:T(8,128)(2,1)S(1)}, bf16[1,256,6,128]{3,1,2,0:T(8,128)(2,1)S(1)}, u32[]{:S(2)}, u32[]{:S(2)}) %collective-permute-start) | collective-permute-done | bytes 393248 | tf_op jit(solution)/shard_map/ppermute | solution.py:12
  32.4 5.3 %collective-permute-done.1 = bf16[1,256,6,128]{3,1,2,0:T(8,128)(2,1)S(1)} collective-permute-done((bf16[1,256,6,128]{3,1,2,0:T(8,128)(2,1)S(1)}, bf16[1,256,6,128]{3,1,2,0:T(8,128)(2,1)S(1)}, u32[]{:S(2)}, u32[]{:S(2)}) %collective-permute-start.1) | collective-permute-done | bytes 393248 | tf_op jit(solution)/shard_map/ppermute | solution.py:15
  37.7 1.7 %select_maximum_fusion = bf16[3,256,8,130]{3,1,2,0:T(8,128)(2,1)S(1)} fusion(bf16[1,256,6,128]{3,1,2,0:T(8,128)(2,1)S(1)} %collective-permute-done.1, bf16[1,256,6,128]{3,1,2,0:T(8,128)(2,1)S(1)} %bitcast.298, bf16[1,256,6,128]{3,1,2,0:T(8,128)(2,1)S(1)} %collective-permute-done), kind=kLoop, calls=%fused_computation.8 | loop fusion | flops 15175680 | bytes 2777088 | tf_op jit(solution)/shard_map/concatenate | solution.py:16
  39.5 0.2 fusion.31
  39.7 0.2 fusion.30
  40.1 0.2 fusion.28
  40.5 0.2 fusion.26
  40.7 0.2 fusion.25
  41.1 0.2 fusion.23
  41.3 0.2 fusion.22
  42.1 0.2 fusion.18
  42.3 0.2 fusion.17
  42.7 0.2 fusion.15
  42.9 0.2 fusion.14
  43.3 0.2 fusion.12
  43.9 0.2 fusion.9
  44.2 43.2 %copy.129 = bf16[1,256,27,6,128]{4,3,2,1,0:T(8,128)(2,1)S(1)} copy(bf16[1,256,27,6,128]{4,1,3,2,0:T(8,128)(2,1)S(1)} %fusion.9) | data formatting | bytes 21233664 | tf_op jit(solution)/shard_map/stack | solution.py:69
  87.3 6.4 %copy.252 = bf16[864,8,6,128]{3,1,2,0:T(8,128)(2,1)} copy(bf16[864,8,6,128]{3,2,1,0:T(8,128)(2,1)S(1)} %bitcast.288) | data formatting | bytes 21233664
  93.8 13.9 %copy.130 = bf16[768,6912]{1,0:T(8,128)(2,1)} copy(bf16[768,6912]{0,1:T(8,128)(2,1)} %bitcast.289) | data formatting | bytes 21233664 | tf_op jit(solution)/shard_map/fwh,wb->fbh/dot_general | solution.py:71
  107.7 2.7 %copy.131 = bf16[256,27,128]{2,1,0:T(8,128)(2,1)S(1)} copy(bf16[256,27,128]{2,0,1:T(8,128)(2,1)} %all-gather.2.cloned.1.call-done) | data formatting | bytes 3538944 | tf_op jit(solution)/shard_map/all_gather | solution.py:92
  110.3 1.6 %reshape.119 = bf16[6912,128,1]{1,0,2:T(8,128)(2,1)} reshape(bf16[256,27,128]{2,1,0:T(8,128)(2,1)S(1)} %copy.131) | data formatting | bytes 3538944 | tf_op jit(solution)/shard_map/reshape | solution.py:70
  111.9 7.4 %fusion.7 = bf16[6,128,128]{2,1,0:T(8,128)(2,1)S(1)} fusion(bf16[6,128,6912]{2,1,0:T(8,128)(2,1)} %bitcast.292, bf16[6912,128,1]{1,0,2:T(8,128)(2,1)} %reshape.119, f32[128]{0:T(128)S(1)} %copy-done.1), kind=kOutput, calls=%fused_computation.15 | convolution fusion | flops 1359249408 | bytes 12583424 | tf_op jit(solution)/shard_map/fwh,wb->fbh/dot_general | solution.py:71
  119.3 0.9 fusion.59
  120.2 0.4 fusion.65
  121.2 1.9 %collective-permute-start.2 = (bf16[1,128,6,128]{1,3,2,0:T(8,128)(2,1)S(1)}, bf16[1,128,6,128]{1,3,2,0:T(8,128)(2,1)S(1)}, u32[]{:S(2)}, u32[]{:S(2)}) collective-permute-start(bf16[1,128,6,128]{1,3,2,0:T(8,128)(2,1)S(1)} %bitcast.303), channel_id=1, source_target_pairs={{1,0},{2,1},{3,2},{4,3},{5,4},{6,5},{7,6},{8,7},{9,8},{10,9},{11,1... | collective-permute-start | bytes 589832 | tf_op jit(solution)/shard_map/ppermute | solution.py:23
  123.9 5.2 %collective-permute-done.2 = bf16[1,128,6,128]{1,3,2,0:T(8,128)(2,1)S(1)} collective-permute-done((bf16[1,128,6,128]{1,3,2,0:T(8,128)(2,1)S(1)}, bf16[1,128,6,128]{1,3,2,0:T(8,128)(2,1)S(1)}, u32[]{:S(2)}, u32[]{:S(2)}) %collective-permute-start.2) | collective-permute-done | bytes 196640 | tf_op jit(solution)/shard_map/ppermute | solution.py:23
  129.0 0.9 fusion.57
  130.7 1.2 copy.161
  131.9 1.4 %copy.162 = bf16[2,64,12,256]{3,1,2,0:T(8,128)(2,1)} copy(bf16[2,64,12,256]{1,3,2,0:T(8,128)(2,1)S(1)} %bitcast.295) | data formatting | bytes 1572864 | tf_op jit(solution)/shard_map/convert_element_type | solution.py:104
  (58 shorter events, 3.4 us)
Async XLA Ops:
  6.5 112.8 %copy-start = (bf16[27,64,128]{2,1,0:T(8,128)(2,1)S(1)}, bf16[27,64,128]{2,1,0:T(8,128)(2,1)}, u32[]{:S(2)}) copy-start(bf16[27,64,128]{2,1,0:T(8,128)(2,1)} %param.7) | copy-start | bytes 1327108
  6.5 101.1 %all-gather.2.cloned.1.call-start = ((), (), s32[]{:S(2)}) async-start(), calls=%async_computation.1 | async-start | bytes 1880064 | tf_op jit(solution)/shard_map/all_gather | solution.py:92
  24.4 8.0 %collective-permute-start = (bf16[1,256,6,128]{3,1,2,0:T(8,128)(2,1)S(1)}, bf16[1,256,6,128]{3,1,2,0:T(8,128)(2,1)S(1)}, u32[]{:S(2)}, u32[]{:S(2)}) collective-permute-start(bf16[1,256,6,128]{3,1,2,0:T(8,128)(2,1)S(1)} %bitcast.296), channel_id=1, source_target_pairs={{0,1},{1,2},{2,3},{3,4},{4,5},{5,6},{6,7},{7,8},{8,9},{9,10},{10,1... | collective-permute-start | bytes 1179656 | tf_op jit(solution)/shard_map/ppermute | solution.py:12
  27.7 10.0 %collective-permute-start.1 = (bf16[1,256,6,128]{3,1,2,0:T(8,128)(2,1)S(1)}, bf16[1,256,6,128]{3,1,2,0:T(8,128)(2,1)S(1)}, u32[]{:S(2)}, u32[]{:S(2)}) collective-permute-start(bf16[1,256,6,128]{3,1,2,0:T(8,128)(2,1)S(1)} %bitcast.297), channel_id=1, source_target_pairs={{1,0},{2,1},{3,2},{4,3},{5,4},{6,5},{7,6},{8,7},{9,8},{10,9},{11,1... | collective-permute-start | bytes 1179656 | tf_op jit(solution)/shard_map/ppermute | solution.py:15
  93.8 18.1 %copy-start.1 = (f32[128]{0:T(128)S(1)}, f32[128]{0:T(128)}, u32[]{:S(2)}) copy-start(f32[128]{0:T(128)} %param.6) | copy-start | bytes 1540
  121.2 7.9 %collective-permute-start.2 = (bf16[1,128,6,128]{1,3,2,0:T(8,128)(2,1)S(1)}, bf16[1,128,6,128]{1,3,2,0:T(8,128)(2,1)S(1)}, u32[]{:S(2)}, u32[]{:S(2)}) collective-permute-start(bf16[1,128,6,128]{1,3,2,0:T(8,128)(2,1)S(1)} %bitcast.303), channel_id=1, source_target_pairs={{1,0},{2,1},{3,2},{4,3},{5,4},{6,5},{7,6},{8,7},{9,8},{10,9},{11,1... | collective-permute-start | bytes 589832 | tf_op jit(solution)/shard_map/ppermute | solution.py:23
Sparse Core Ops, SparseCore 0:
  29.8 39.9 all-gather.1
where the time goes:
time: 141 us; the launch traced here: 140 us
  local copies, waits for them, and re-layouts  76.6 us (54%)
  blocking collectives  17.9 us (13%)
  between operations  13.9 us (10%)
  waiting for transfers between devices  13.2 us (9%)
  matrix products  9.13 us (6%)
  starting transfers between devices  7.09 us (5%)
  other arithmetic  2.26 us (2%)
    another operation x2, local copies, waits for them, and re-layouts, conv_rows(): jnp.stack(taps, axis=2).reshape(count, chans * 27, wide_y * wide_z)  43.4 us
    all_to_all x1, blocking collectives, per_device(): lax.all_to_all(volume, 'gx', split_axis=0, concat_axis=1, tiled=True)  17.9 us
    dot_general x1, local copies, waits for them, and re-layouts, conv_rows(): jnp.einsum('fwh,wb->fbh', patch_columns, flattened_patches, preferred_ele...  13.9 us
    unnamed x32, local copies, waits for them, and re-layouts  10.8 us
    dot_general x1, matrix products, conv_rows(): jnp.einsum('fwh,wb->fbh', patch_columns, flattened_patches, preferred_ele...  7.43 us
    ppermute x1, waiting for transfers between devices, extended(): lax.ppermute(lax.slice_in_dim(block, 0, width, axis=dim), axis, backward)  5.28 us
    ppermute x1, waiting for transfers between devices, from_behind(): return lax.ppermute(block, axis, route)  5.16 us
    ppermute x1, starting transfers between devices, extended(): lax.ppermute(lax.slice_in_dim(block, block.shape[dim] - width, None, axis...  3.24 us
  transfers between devices with their start and end apart: 4, of which 3 were waited for; matrix products, arithmetic and copies ran while one was open for 50% of the time, Pallas kernels for 0%

commit v1 on v0

--- a/solution.py
+++ b/solution.py
@@ -86,7 +86,10 @@
     wide_x, wide_y, wide_z = (volume.shape[0], volume.shape[2], volume.shape[3])
     rows = wide_x // lax.axis_size("gx")
     cout = conv_weight.shape[2]
-    local = lax.all_to_all(volume, "gx", split_axis=0, concat_axis=1, tiled=True)
+    local = jnp.concatenate(
+        lax.all_to_all(jnp.stack(jnp.split(volume, lax.axis_size("gx"), axis=0)), "gx", 0, 0),
+        axis=1,
+    )
     widened_volume = extended(local, (("gx", 0),), 1)
     padded_volume = jnp.pad(widened_volume, ((0, 0), (0, 0), (1, 1), (1, 1)))
     summed = conv_rows(padded_volume, lax.all_gather(conv_weight, "gx", axis=0, tiled=True), rows)

time: 141 us -> 153 us (1.085)
  local copies, waits for them, and re-layouts: 76.6 us -> 88.6 us
    unnamed x32 -> x47, local copies, waits for them, and re-layouts: 10.8 us -> 22 us
  transfers between devices with their start and end apart: 4 -> 4, of which waited for: 3 -> 3; matrix products, arithmetic and copies ran while one was open for 50% -> 46% of each run, Pallas kernels for 0% -> 0%
where the time goes in v1:
time: 153 us; the launch traced here: 152 us
  local copies, waits for them, and re-layouts  88.6 us (58%)
  blocking collectives  17.5 us (11%)
  between operations  14 us (9%)
  waiting for transfers between devices  13.2 us (9%)
  matrix products  9.13 us (6%)
  starting transfers between devices  7.09 us (5%)
  other arithmetic  2.26 us (1%)
    another operation x2, local copies, waits for them, and re-layouts, conv_rows(): jnp.stack(taps, axis=2).reshape(count, chans * 27, wide_y * wide_z)  43.4 us
    unnamed x47, local copies, waits for them, and re-layouts  22 us
    all_to_all x1, blocking collectives, per_device(): lax.all_to_all(jnp.stack(jnp.split(volume, lax.axis_size('gx'), axis=0)),...  17.5 us
    dot_general x1, local copies, waits for them, and re-layouts, conv_rows(): jnp.einsum('fwh,wb->fbh', patch_columns, flattened_patches, preferred_ele...  13.9 us
    dot_general x1, matrix products, conv_rows(): jnp.einsum('fwh,wb->fbh', patch_columns, flattened_patches, preferred_ele...  7.43 us
    ppermute x1, waiting for transfers between devices, extended(): lax.ppermute(lax.slice_in_dim(block, 0, width, axis=dim), axis, backward)  5.28 us
    ppermute x1, waiting for transfers between devices, from_behind(): return lax.ppermute(block, axis, route)  5.16 us
    ppermute x1, starting transfers between devices, extended(): lax.ppermute(lax.slice_in_dim(block, block.shape[dim] - width, None, axis...  3.24 us
  transfers between devices with their start and end apart: 4, of which 3 were waited for; matrix products, arithmetic and copies ran while one was open for 46% of the time, Pallas kernels for 0%

profile of v1, /device:TPU:5, one launch (start us, length us, event | category | flops | bytes accessed | tf_op | source)
XLA Modules:
  0.0 151.8 jit_solution(498744873498025967)
XLA Ops:
  6.5 0.8 constant_dynamic-update-slice_fusion.15
  7.3 0.7 constant_dynamic-update-slice_fusion.14
  8.1 0.7 constant_dynamic-update-slice_fusion.13
  8.8 0.7 constant_dynamic-update-slice_fusion.12
  9.6 0.7 constant_dynamic-update-slice_fusion.11
  10.3 0.7 constant_dynamic-update-slice_fusion.10
  11.1 0.7 constant_dynamic-update-slice_fusion.9
  11.8 0.7 constant_dynamic-update-slice_fusion.8
  13.3 0.7 constant_dynamic-update-slice_fusion.6
  14.0 0.7 constant_dynamic-update-slice_fusion.5
  14.8 0.7 constant_dynamic-update-slice_fusion.4
  15.5 0.7 constant_dynamic-update-slice_fusion.3
  16.3 0.7 constant_dynamic-update-slice_fusion.2
  17.8 0.7 constant_dynamic-update-slice_fusion
  18.5 17.5 %all_to_all.5 = bf16[16,1,16,6,128]{4,2,3,1,0:T(8,128)(2,1)S(1)} all-to-all(bf16[16,1,16,6,128]{4,2,3,1,0:T(8,128)(2,1)S(1)} %constant_dynamic-update-slice_fusion), channel_id=1, replica_groups=mesh['groups'=2,'gx'=16] {'gx'}, dimensions={0} | all-to-all | bytes 786432 | tf_op jit(solution)/shard_map/all_to_all | solution.py:90
  36.1 3.2 %collective-permute-start = (bf16[1,256,6,128]{3,1,2,0:T(8,128)(2,1)S(1)}, bf16[1,256,6,128]{3,1,2,0:T(8,128)(2,1)S(1)}, u32[]{:S(2)}, u32[]{:S(2)}) collective-permute-start(bf16[1,256,6,128]{3,1,2,0:T(8,128)(2,1)S(1)} %bitcast.328), channel_id=1, source_target_pairs={{0,1},{1,2},{2,3},{3,4},{4,5},{5,6},{6,7},{7,8},{8,9},{9,10},{10,1... | collective-permute-start | bytes 1179656 | tf_op jit(solution)/shard_map/ppermute | solution.py:12
  39.3 1.9 %collective-permute-start.1 = (bf16[1,256,6,128]{3,1,2,0:T(8,128)(2,1)S(1)}, bf16[1,256,6,128]{3,1,2,0:T(8,128)(2,1)S(1)}, u32[]{:S(2)}, u32[]{:S(2)}) collective-permute-start(bf16[1,256,6,128]{3,1,2,0:T(8,128)(2,1)S(1)} %bitcast.329), channel_id=1, source_target_pairs={{1,0},{2,1},{3,2},{4,3},{5,4},{6,5},{7,6},{8,7},{9,8},{10,9},{11,1... | collective-permute-start | bytes 1179656 | tf_op jit(solution)/shard_map/ppermute | solution.py:15
  41.3 2.8 %collective-permute-done = bf16[1,256,6,128]{3,1,2,0:T(8,128)(2,1)S(1)} collective-permute-done((bf16[1,256,6,128]{3,1,2,0:T(8,128)(2,1)S(1)}, bf16[1,256,6,128]{3,1,2,0:T(8,128)(2,1)S(1)}, u32[]{:S(2)}, u32[]{:S(2)}) %collective-permute-start) | collective-permute-done | bytes 393248 | tf_op jit(solution)/shard_map/ppermute | solution.py:12
  44.0 5.3 %collective-permute-done.1 = bf16[1,256,6,128]{3,1,2,0:T(8,128)(2,1)S(1)} collective-permute-done((bf16[1,256,6,128]{3,1,2,0:T(8,128)(2,1)S(1)}, bf16[1,256,6,128]{3,1,2,0:T(8,128)(2,1)S(1)}, u32[]{:S(2)}, u32[]{:S(2)}) %collective-permute-start.1) | collective-permute-done | bytes 393248 | tf_op jit(solution)/shard_map/ppermute | solution.py:15
  49.3 1.7 %select_maximum_fusion = bf16[3,256,8,130]{3,1,2,0:T(8,128)(2,1)S(1)} fusion(bf16[1,256,6,128]{3,1,2,0:T(8,128)(2,1)S(1)} %collective-permute-done.1, bf16[1,256,6,128]{3,1,2,0:T(8,128)(2,1)S(1)} %bitcast.330, bf16[1,256,6,128]{3,1,2,0:T(8,128)(2,1)S(1)} %collective-permute-done), kind=kLoop, calls=%fused_computation.8 | loop fusion | flops 15175680 | bytes 2777088 | tf_op jit(solution)/shard_map/concatenate | solution.py:16
  55.8 43.2 %copy.127 = bf16[1,256,27,6,128]{4,3,2,1,0:T(8,128)(2,1)S(1)} copy(bf16[1,256,27,6,128]{4,1,3,2,0:T(8,128)(2,1)S(1)} %fusion.9) | data formatting | bytes 21233664 | tf_op jit(solution)/shard_map/stack | solution.py:69
  99.0 6.4 %copy.250 = bf16[864,8,6,128]{3,1,2,0:T(8,128)(2,1)} copy(bf16[864,8,6,128]{3,2,1,0:T(8,128)(2,1)S(1)} %bitcast.320) | data formatting | bytes 21233664
  105.4 13.9 %copy.128 = bf16[768,6912]{1,0:T(8,128)(2,1)} copy(bf16[768,6912]{0,1:T(8,128)(2,1)} %bitcast.321) | data formatting | bytes 21233664 | tf_op jit(solution)/shard_map/fwh,wb->fbh/dot_general | solution.py:71
  119.3 2.7 %copy.129 = bf16[256,27,128]{2,1,0:T(8,128)(2,1)S(1)} copy(bf16[256,27,128]{2,0,1:T(8,128)(2,1)} %all-gather.2.cloned.1.call-done) | data formatting | bytes 3538944 | tf_op jit(solution)/shard_map/all_gather | solution.py:95
  122.0 1.6 %reshape.120 = bf16[6912,128,1]{1,0,2:T(8,128)(2,1)} reshape(bf16[256,27,128]{2,1,0:T(8,128)(2,1)S(1)} %copy.129) | data formatting | bytes 3538944 | tf_op jit(solution)/shard_map/reshape | solution.py:70
  123.5 7.4 %fusion.7 = bf16[6,128,128]{2,1,0:T(8,128)(2,1)S(1)} fusion(bf16[6,128,6912]{2,1,0:T(8,128)(2,1)} %bitcast.324, bf16[6912,128,1]{1,0,2:T(8,128)(2,1)} %reshape.120, f32[128]{0:T(128)S(1)} %copy-done.1), kind=kOutput, calls=%fused_computation.15 | convolution fusion | flops 1359249408 | bytes 12583424 | tf_op jit(solution)/shard_map/fwh,wb->fbh/dot_general | solution.py:71
  130.9 0.9 fusion.59
  132.8 1.9 %collective-permute-start.2 = (bf16[1,128,6,128]{1,3,2,0:T(8,128)(2,1)S(1)}, bf16[1,128,6,128]{1,3,2,0:T(8,128)(2,1)S(1)}, u32[]{:S(2)}, u32[]{:S(2)}) collective-permute-start(bf16[1,128,6,128]{1,3,2,0:T(8,128)(2,1)S(1)} %bitcast.335), channel_id=1, source_target_pairs={{1,0},{2,1},{3,2},{4,3},{5,4},{6,5},{7,6},{8,7},{9,8},{10,9},{11,1... | collective-permute-start | bytes 589832 | tf_op jit(solution)/shard_map/ppermute | solution.py:23
  135.5 5.2 %collective-permute-done.2 = bf16[1,128,6,128]{1,3,2,0:T(8,128)(2,1)S(1)} collective-permute-done((bf16[1,128,6,128]{1,3,2,0:T(8,128)(2,1)S(1)}, bf16[1,128,6,128]{1,3,2,0:T(8,128)(2,1)S(1)}, u32[]{:S(2)}, u32[]{:S(2)}) %collective-permute-start.2) | collective-permute-done | bytes 196640 | tf_op jit(solution)/shard_map/ppermute | solution.py:23
  140.7 0.9 fusion.57
  142.4 1.2 copy.159
  143.5 1.4 copy.160
  (74 shorter events, 8.4 us)
Async XLA Ops:
  6.5 124.4 %copy-start = (bf16[27,64,128]{2,1,0:T(8,128)(2,1)S(1)}, bf16[27,64,128]{2,1,0:T(8,128)(2,1)}, u32[]{:S(2)}) copy-start(bf16[27,64,128]{2,1,0:T(8,128)(2,1)} %param.7) | copy-start | bytes 1327108
  6.5 112.8 %all-gather.2.cloned.1.call-start = ((), (), s32[]{:S(2)}) async-start(), calls=%async_computation.1 | async-start | bytes 1880064 | tf_op jit(solution)/shard_map/all_gather | solution.py:95
  36.1 8.0 %collective-permute-start = (bf16[1,256,6,128]{3,1,2,0:T(8,128)(2,1)S(1)}, bf16[1,256,6,128]{3,1,2,0:T(8,128)(2,1)S(1)}, u32[]{:S(2)}, u32[]{:S(2)}) collective-permute-start(bf16[1,256,6,128]{3,1,2,0:T(8,128)(2,1)S(1)} %bitcast.328), channel_id=1, source_target_pairs={{0,1},{1,2},{2,3},{3,4},{4,5},{5,6},{6,7},{7,8},{8,9},{9,10},{10,1... | collective-permute-start | bytes 1179656 | tf_op jit(solution)/shard_map/ppermute | solution.py:12
  39.3 10.0 %collective-permute-start.1 = (bf16[1,256,6,128]{3,1,2,0:T(8,128)(2,1)S(1)}, bf16[1,256,6,128]{3,1,2,0:T(8,128)(2,1)S(1)}, u32[]{:S(2)}, u32[]{:S(2)}) collective-permute-start(bf16[1,256,6,128]{3,1,2,0:T(8,128)(2,1)S(1)} %bitcast.329), channel_id=1, source_target_pairs={{1,0},{2,1},{3,2},{4,3},{5,4},{6,5},{7,6},{8,7},{9,8},{10,9},{11,1... | collective-permute-start | bytes 1179656 | tf_op jit(solution)/shard_map/ppermute | solution.py:15
  105.4 18.1 %copy-start.1 = (f32[128]{0:T(128)S(1)}, f32[128]{0:T(128)}, u32[]{:S(2)}) copy-start(f32[128]{0:T(128)} %param.6) | copy-start | bytes 1540
  132.8 7.9 %collective-permute-start.2 = (bf16[1,128,6,128]{1,3,2,0:T(8,128)(2,1)S(1)}, bf16[1,128,6,128]{1,3,2,0:T(8,128)(2,1)S(1)}, u32[]{:S(2)}, u32[]{:S(2)}) collective-permute-start(bf16[1,128,6,128]{1,3,2,0:T(8,128)(2,1)S(1)} %bitcast.335), channel_id=1, source_target_pairs={{1,0},{2,1},{3,2},{4,3},{5,4},{6,5},{7,6},{8,7},{9,8},{10,9},{11,1... | collective-permute-start | bytes 589832 | tf_op jit(solution)/shard_map/ppermute | solution.py:23
Sparse Core Ops, SparseCore 0:
  41.4 39.9 all-gather.1
